TPU v7x, 32 devices: a whole 2x2x4 slice. The times are simulated.
32 devices in a mesh: dp: 4 (over y, core), ctx: 8 (over z, x).
Axes of the slice: x: 2, y: 2, z: 4, core: 2. Of those that a mesh axis runs over, the one named last changes fastest.
Arguments:
- features: bfloat16 [4, 8, 248, 12288], P('dp', 'ctx'), may hold values from -6 to 6
- counts: int32 [4, 8], P('dp', 'ctx'), may hold values from 8 to 248, as said below
- short_taps: float32 [7, 3, 4096], P(None, None, 'ctx'), may hold values from -2 to 2
- residue: float32 [16, 256], P(None, 'ctx'), may hold values from -0.25 to 0.25
- decay_rate: float32 [16, 256], P(None, 'ctx'), may hold values from 1.953125e-05 to 0.05
- skip_gain: float32 [4096], P('ctx'), may hold values from -4 to 4
- cotangent: bfloat16 [4, 8, 248, 4096], P('dp', 'ctx'), may hold values from -6 to 6
Outputs:
- output: bfloat16 [4, 8, 248, 4096], P('dp', 'ctx')
- grad_features: bfloat16 [4, 8, 248, 12288], P('dp', 'ctx')
- grad_taps: float32 [7, 3, 4096], P(None, None, 'ctx')
- grad_residue: float32 [16, 256], P(None, 'ctx')
- grad_skip: float32 [4096], P('ctx')
Inputs may be any that keep to these rules, and one draw needn't show every extreme that they name: Along ctx the loader shards come in pairs 2m, 2m + 1 whose counts sum to 256; each replica has a shard holding exactly 248 rows; the counts of a replica sum to 1024.
All inputs are finite; a program needn't handle non-finite values.
Results may differ from a plain program's by a relative error of at most 0.0069.
Values may be sent and summed in bfloat16 or wider, within the bound.
A program may use at most 128 MiB of HBM per device.

v0:
```python
import jax
import jax.numpy as jnp
from jax import lax
from jax.sharding import PartitionSpec as P

TAPS = 7
TOK_DEV = 128


def modal_local(mixed, d_long, residue, decay_rate, row_block):
    highest = lax.Precision.HIGHEST
    length, channels = mixed.shape
    groups = residue.shape[1]
    group_size = channels // groups
    block_count = length // row_block
    lag_steps = jnp.arange(row_block, dtype=jnp.float32)
    decay_col = decay_rate[:, :, None]
    lag_powers = jnp.exp(-decay_col * lag_steps)
    kernel_rows = jnp.sum(residue[:, :, None] * lag_powers, axis=0)
    lag_int = jnp.arange(row_block, dtype=jnp.int32)
    lag_grid = lag_int[:, None] - lag_int[None, :]
    lower_part = lag_grid >= 0
    toeplitz = jnp.where(
        lower_part[None], jnp.take(kernel_rows, jnp.clip(lag_grid, 0, row_block - 1), axis=1), 0.0
    )
    out_powers = jnp.exp(-decay_col * (lag_steps + 1.0))
    in_powers = jnp.exp(-decay_col * (row_block - 1.0 - lag_steps))
    res_out = residue[:, :, None] * out_powers
    block_ids = jnp.arange(block_count, dtype=jnp.float32)
    block_gap = block_ids[:, None] - 1.0 - block_ids[None, :]
    carry_decay = jnp.where(
        block_gap >= 0.0,
        jnp.exp(-decay_rate[:, :, None, None] * row_block * jnp.maximum(block_gap, 0.0)),
        0.0,
    )
    lag_float = jnp.maximum(lag_grid, 0).astype(jnp.float32)
    mixed_blocks = mixed.reshape(block_count, row_block, groups, group_size)
    grad_blocks = d_long.reshape(block_count, row_block, groups, group_size)
    intra = jnp.einsum("gab,nbgq->nagq", toeplitz, mixed_blocks, precision=highest)
    local_state = jnp.einsum("rgb,nbgq->nrgq", in_powers, mixed_blocks, precision=highest)
    cross_state = jnp.einsum("rgij,jrgq->irgq", carry_decay, local_state, precision=highest)
    cross = jnp.einsum("rga,irgq->iagq", res_out, cross_state, precision=highest)
    long_part = (intra + cross).reshape(length, channels)
    du_intra = jnp.einsum("gab,nagq->nbgq", toeplitz, grad_blocks, precision=highest)
    d_cross = jnp.einsum("rga,iagq->irgq", res_out, grad_blocks, precision=highest)
    d_local = jnp.einsum("rgij,irgq->jrgq", carry_decay, d_cross, precision=highest)
    du_cross = jnp.einsum("rgb,nrgq->nbgq", in_powers, d_local, precision=highest)
    mixed_part = (du_intra + du_cross).reshape(length, channels)
    pair_sums = jnp.einsum("nagq,nbgq->gab", grad_blocks, mixed_blocks, precision=highest)

    def one_pole(pole_rates):
        weight = jnp.where(
            lower_part[None], jnp.exp(-pole_rates[:, None, None] * lag_float[None]), 0.0
        )
        return jnp.sum(pair_sums * weight, axis=(1, 2))

    grad_res = lax.map(one_pole, decay_rate)
    grad_res = grad_res + jnp.einsum(
        "iagq,rga,irgq->rg", grad_blocks, out_powers, cross_state, precision=highest
    )
    return (long_part, mixed_part, grad_res)


def moved_operator(features, counts, short_taps, residue, decay_rate, skip_gain, cotangent):
    shards = lax.axis_size("ctx")
    capacity = features.shape[2]
    model_width = cotangent.shape[3]
    channels = short_taps.shape[2]
    window_len = TOK_DEV * shards
    loader_in = features[0, 0].reshape(capacity, 3, model_width)
    cot_rows = cotangent[0, 0].reshape(capacity, 1, model_width)
    slot_ids = jnp.arange(capacity, dtype=jnp.int32)
    all_counts = lax.all_gather(counts, "ctx", axis=1, tiled=True)[0]
    shard_ends = jnp.cumsum(all_counts)
    shard_starts = shard_ends - all_counts
    positions = jnp.arange(window_len, dtype=jnp.int32)
    passed = shard_ends[None, :] <= positions[:, None]
    shard_of = jnp.sum(passed.astype(jnp.int32), axis=1)
    before = jnp.sum(jnp.where(passed, all_counts[None, :], 0), axis=1)
    take_index = shard_of * capacity + positions - before
    back_index = jnp.clip(shard_starts[:, None] + slot_ids[None, :], 0, window_len - 1).reshape(-1)
    back_valid = (slot_ids[None, :] < all_counts[:, None]).reshape(-1)

    def place(received):
        return jnp.take(received, take_index, axis=0)

    def inbound(loader_rows):
        return place(lax.all_to_all(loader_rows, "ctx", split_axis=2, concat_axis=0, tiled=True))

    def outbound(chan_rows):
        picked = jnp.take(chan_rows, back_index, axis=0)
        picked = jnp.where(back_valid[:, None, None], picked, jnp.zeros_like(picked))
        return lax.all_to_all(picked, "ctx", split_axis=0, concat_axis=2, tiled=True)

    window = inbound(loader_in)
    grad_chan = inbound(cot_rows)[:, 0, :]
    padded = jnp.pad(window, ((TAPS - 1, 0), (0, 0), (0, 0)))
    short_out = jnp.zeros((window_len, 3, channels), jnp.float32)
    for tap_index in range(TAPS):
        piece = padded[TAPS - 1 - tap_index : TAPS - 1 - tap_index + window_len].astype(jnp.float32)
        short_out = short_out + short_taps[tap_index] * piece
    short_b = short_out.astype(jnp.bfloat16)
    query_f = short_b[:, 0].astype(jnp.float32)
    key_f = short_b[:, 1].astype(jnp.float32)
    value_f = short_b[:, 2].astype(jnp.float32)
    mixed = (key_f * value_f).astype(jnp.bfloat16).astype(jnp.float32)
    grad_f = grad_chan.astype(jnp.float32)
    d_long = grad_f * query_f
    long_part, mixed_part, grad_res = modal_local(mixed, d_long, residue, decay_rate, 128)
    long_out = long_part + skip_gain * mixed
    gated = (query_f * long_out).astype(jnp.bfloat16)
    gated_rows = outbound(gated[:, None, :])
    d_query = grad_f * long_out
    d_mixed = mixed_part + skip_gain * d_long
    grad_gain = jnp.sum(d_long * mixed, axis=0)
    d_short = jnp.stack([d_query, d_mixed * value_f, d_mixed * key_f], axis=1)
    tail = jnp.pad(d_short, ((0, TAPS - 1), (0, 0), (0, 0)))
    d_window = jnp.zeros((window_len, 3, channels), jnp.float32)
    tap_grads = []
    for tap_index in range(TAPS):
        d_window = d_window + short_taps[tap_index] * tail[tap_index : tap_index + window_len]
        piece = padded[TAPS - 1 - tap_index : TAPS - 1 - tap_index + window_len].astype(jnp.float32)
        tap_grads.append(jnp.sum(d_short * piece, axis=0))
    grad_rows = outbound(d_window.astype(jnp.bfloat16))
    return (
        gated_rows.reshape(1, 1, capacity, model_width),
        grad_rows.reshape(1, 1, capacity, 3 * model_width),
        jnp.stack(tap_grads, axis=0),
        grad_res,
        grad_gain,
    )


def per_device(features, counts, short_taps, residue, decay_rate, skip_gain, cotangent):
    results = moved_operator(
        features, counts, short_taps, residue, decay_rate, skip_gain, cotangent
    )
    grad_tap, grad_res, grad_gain = lax.psum((results[2], results[3], results[4]), "dp")
    return (results[0], results[1], grad_tap, grad_res, grad_gain)


def solution(mesh):
    in_specs = (
        P("dp", "ctx", None, None),
        P("dp", "ctx"),
        P(None, None, "ctx"),
        P(None, "ctx"),
        P(None, "ctx"),
        P("ctx"),
        P("dp", "ctx", None, None),
    )
    out_specs = (
        P("dp", "ctx", None, None),
        P("dp", "ctx", None, None),
        P(None, None, "ctx"),
        P(None, "ctx"),
        P("ctx"),
    )
    return jax.shard_map(
        per_device, mesh=mesh, in_specs=in_specs, out_specs=out_specs, check_vma=False
    )
```

profile of v0, /device:TPU:0, one launch (start us, length us, event | category | flops | bytes accessed | tf_op | source)
XLA Modules:
  0.0 809.5 jit_solution(16444914577203407402)
XLA Ops:
  0.6 10.0 %copy.211 = bf16[248,1,4096]{0,1,2:T(2,128)(2,1)} copy(bf16[248,1,4096]{2,0,1:T(8,128)(2,1)} %bitcast.210) | data formatting | bytes 4063232 | tf_op jit(solution)/shard_map/reshape;squeeze | solution.py:71
  11.1 23.6 %reduce.2 = bf16[4096,248]{1,0:T(8,128)(2,1)S(1)} reduce(bf16[4096,1,248]{2,1,0:T(2,128)(2,1)} %bitcast.196, bf16[]{:T(256)} %broadcast.388), dimensions={1}, to_apply=%bitcast.179.reduce_sub_computation | reduce | bytes 4063234
  34.7 6.0 reshape.459
  40.8 7.3 all-to-all-start.2
  48.0 8.4 %copy.192 = bf16[1,1,248,12288]{2,3,1,0:T(8,128)(2,1)} copy(bf16[1,1,248,12288]{3,2,1,0:T(8,128)(2,1)} %param.9) | data formatting | bytes 12189696 | tf_op args[0]
  56.5 10.4 %copy.193 = bf16[248,3,4096]{0,1,2:T(4,128)(2,1)} copy(bf16[248,3,4096]{0,2,1:T(8,128)(2,1)} %bitcast.192) | data formatting | bytes 12189696 | tf_op jit(solution)/shard_map/reshape;squeeze | solution.py:70
  66.9 27.9 %all-to-all-done.2 = bf16[8,2,63488]{2,1,0:T(2,128)(2,1)S(1)} async-done(((bf16[8,2,63488]{2,1,0:T(2,128)(2,1)}), bf16[8,2,63488]{2,1,0:T(2,128)(2,1)S(1)}, u32[]{:S(2)}, u32[]{:S(2)}) %all-to-all-start.2) | async-done | bytes 2031648 | tf_op jit(solution)/shard_map/all_to_all | solution.py:88
  94.9 5.0 all-to-all-start
  101.8 180.5 %all-reduce.2 = s32[8]{0:T(128)S(1)} all-reduce(s32[8]{0:T(128)S(1)} %bitcast_dynamic-update-slice_fusion), channel_id=1, replica_groups=mesh['dp'=4,'ctx'=8] {'ctx'}, use_global_device_ids=true, to_apply=%add.2 | all-reduce | flops 8 | bytes 64 | tf_op jit(solution)/shard_map/lt | solution.py:82
  283.5 54.4 %gather_fusion.1 = f32[16384,32]{1,0:T(8,128)} fusion(f32[32,128]{0,1:T(8,128)S(1)} %copy.201, s32[16384]{0:T(1024)S(1)} %fusion.91), kind=kCustom, calls=%fused_computation.1 | custom fusion | bytes 4259840 | tf_op jit(solution)/shard_map/jit(_take)/gather | solution.py:24
  337.9 6.5 copy.202
  344.9 8.7 %reshape.460 = bf16[4096,1,248]{2,1,0:T(2,128)(2,1)} reshape(bf16[8,2,63488]{2,1,0:T(2,128)(2,1)S(1)} %all-to-all-done.2) | data formatting | bytes 4063232
  366.6 13.0 %copy.239 = bf16[248,3,8,512]{3,0,2,1:T(8,128)(2,1)} copy(bf16[248,3,8,512]{0,1,3,2:T(4,128)(2,1)} %bitcast.6) | data formatting | bytes 12189696 | tf_op jit(solution)/shard_map/all_to_all | solution.py:88
  379.6 23.3 %copy.196 = bf16[1984,3,512]{2,1,0:T(4,128)(2,1)} copy(bf16[1984,3,512]{2,0,1:T(8,128)(2,1)} %bitcast.193) | data formatting | bytes 12189696 | tf_op jit(solution)/shard_map/all_to_all | solution.py:88
  402.9 14.0 %gather_fusion = bf16[1024,3,512]{2,1,0:T(4,128)(2,1)} fusion(bf16[1984,3,512]{2,1,0:T(4,128)(2,1)} %copy.196, s32[1024]{0:T(1024)S(1)} %broadcast_clamp_fusion), kind=kCustom, calls=%fused_computation | custom fusion | bytes 6295552 | tf_op jit(solution)/shard_map/jit(_take)/gather | solution.py:85
  420.0 5.8 fusion.11
  472.6 5.7 fusion.42
  490.6 6.1 convert_multiply_fusion.15
  496.8 9.2 %gather_fusion.2 = bf16[1984,512]{1,0:T(8,128)(2,1)} fusion(bf16[1024,512]{1,0:T(8,128)(2,1)S(1)} %get-tuple-element.108, s32[2048]{0:T(1024)S(1)} %pad_clamp_fusion), kind=kCustom, calls=%fused_computation.2 | custom fusion | bytes 4071168 | tf_op jit(solution)/shard_map/jit(_take)/gather | solution.py:91
  514.2 5.9 reshape.457
  524.4 13.9 %fusion.18 = (f32[3,512]{1,0:T(4,128)S(1)}, f32[3,512]{1,0:T(4,128)S(1)}, f32[3,512]{1,0:T(4,128)S(1)}, f32[3,512]{1,0:T(4,128)S(1)}, f32[3,512]{1,0:T(4,128)S(1...) fusion(bf16[1024,3,512]{2,0,1:T(8,128)(2,1)} %copy-done.3, ...), kind=kLoop, calls=%fused_computation.40 | loop fusion | flops 36165120 | bytes 15771648 | tf_op jit(solution)/shard_map/reduce_sum | solution.py:123
  538.3 5.2 add_convert_fusion
  548.3 23.6 %gather_fusion.4 = bf16[1984,3,512]{2,1,0:T(4,128)(2,1)} fusion(bf16[1024,3,512]{2,1,0:T(4,128)(2,1)} %copy.222, s32[2048]{0:T(1024)S(1)} %pad_clamp_fusion), kind=kCustom, calls=%fused_computation.4 | custom fusion | bytes 12197632 | tf_op jit(solution)/shard_map/jit(_take)/gather | solution.py:91
  571.9 16.4 %fusion.25 = f32[16,32]{0,1:T(8,128)S(1)} fusion(f32[16,32,8,16]{3,2,1,0:T(8,128)} %bitcast.195, f32[8,128,32,16]{1,0,3,2:T(8,128)S(1)} %convert_multiply_fusion.20, f32[128]{0:T(128)S(1)} %iota_add_fusion, f32[16,32]{0,1:T(8,128)S(1)} %copy.200), kind=kOutput, calls=%fused_computation.59 | convolution fusion | flops 100859392 | bytes 2363904 | tf_op jit(solution)/shard_map/iagq,rga,irgq->rg/dot_general | solution.py:58
  592.6 11.9 %select_select_fusion = bf16[1984,3,512]{2,1,0:T(4,128)(2,1)} fusion(bf16[1984,3,512]{2,1,0:T(4,128)(2,1)S(1)} %copy-done.2, pred[1984]{0:T(1024)(128)(4,1)S(1)} %compare_and_fusion, pred[1984]{0:T(1024)(128)(4,1)S(1)} %lt.99), kind=kLoop, calls=%fused_computation.12 | loop fusion | flops 6094848 | bytes 12193664 | tf_op jit(solution)/shard_map/jit(_where)/select_n | solution.py:92
  604.5 5.9 all-to-all-start.3
  610.4 11.9 %while.11 = (s32[]{:T(128)}, f32[16,32]{1,0:T(8,128)S(1)}, f32[16,32]{1,0:T(8,128)S(1)}, f32[32,128,128]{2,1,0:T(8,128)S(1)}, s32[]{:T(128)}, /*index=5*/s32[]{:T(128)}) while((s32[]{:T(128)}, f32[16,32]{1,0:T(8,128)S(1)}, f32[16,32]{1,0:T(8,128)S(1)}, f32[32,128,128]{2,1,0:T(8,128)S(1)}, s32[]{:T(128)}, ...), condition=%wide.region_14.15_spmd.clone, body=%wide.region_12.14_spmd.clone.sunk | while | flops 2179074 | bytes 2261845 | solution.py:57
  622.4 12.4 %all-reduce.3 = (f32[7,3,512]{2,1,0:T(4,128)S(1)}, f32[16,32]{1,0:T(8,128)}, f32[512]{0:T(512)}) all-reduce(f32[7,3,512]{2,1,0:T(4,128)S(1)} %constant_dynamic-update-slice_fusion, f32[16,32]{1,0:T(8,128)S(1)} %add.246, f32[512]{0:T(512)S(1)} %get-tuple-element.99), channel_id=1, replica_groups=mesh['dp'=4,'ctx'=8] {'dp'}, use_global_device_ids=true, to_apply=%region_11.12 | all-reduce | flops 11776 | bytes 94208 | tf_op jit(solution)/shard_map/psum | solution.py:138
  635.5 6.8 reshape.458
  647.9 139.1 %all-to-all-done.3 = bf16[1984,3,512]{2,1,0:T(4,128)(2,1)} async-done(((bf16[1984,3,512]{2,1,0:T(4,128)(2,1)}), bf16[1984,3,512]{2,1,0:T(4,128)(2,1)}, u32[]{:S(2)}, u32[]{:S(2)}) %all-to-all-start.3) | async-done | bytes 6094880 | tf_op jit(solution)/shard_map/all_to_all | solution.py:93
  787.0 12.5 %copy.223 = bf16[248,3,8,512]{3,2,1,0:T(8,128)(2,1)} copy(bf16[248,3,8,512]{3,1,0,2:T(4,128)(2,1)} %bitcast.43) | data formatting | bytes 12189696 | tf_op jit(solution)/shard_map/all_to_all | solution.py:93
  799.5 9.8 %reshape.389 = bf16[1,1,248,12288]{3,2,1,0:T(8,128)(2,1)} reshape(bf16[248,3,8,512]{3,2,1,0:T(8,128)(2,1)} %copy.223) | data formatting | bytes 12189696 | tf_op jit(solution)/shard_map/reshape | solution.py:127
  (201 shorter events, 117.7 us)
Async XLA Ops:
  40.8 54.1 %all-to-all-start.2 = ((bf16[8,2,63488]{2,1,0:T(2,128)(2,1)}), bf16[8,2,63488]{2,1,0:T(2,128)(2,1)S(1)}, u32[]{:S(2)}, u32[]{:S(2)}) async-start(bf16[8,2,63488]{2,1,0:T(2,128)(2,1)} %reshape.459), calls=%async_computation.2 | async-start | bytes 4063232 | tf_op jit(solution)/shard_map/all_to_all | solution.py:88
  66.9 33.7 %copy-start.16 = (u32[32]{0:T(128)S(1)}, u32[32]{0:T(128)}, u32[]{:S(2)}) copy-start(u32[32]{0:T(128)} %constant.117) | copy-start | bytes 388
  66.9 215.9 %copy-start.12 = (f32[7,3,512]{2,0,1:T(8,128)S(1)}, f32[7,3,512]{2,0,1:T(8,128)}, u32[]{:S(2)}) copy-start(f32[7,3,512]{2,0,1:T(8,128)} %param.11) | copy-start | bytes 129028
  66.9 216.0 %copy-start.14 = (f32[16,32]{1,0:T(8,128)S(1)}, f32[16,32]{1,0:T(8,128)}, u32[]{:S(2)}) copy-start(f32[16,32]{1,0:T(8,128)} %param.13) | copy-start | bytes 6148
  66.9 216.1 %copy-start.13 = (f32[16,32]{1,0:T(8,128)S(1)}, f32[16,32]{1,0:T(8,128)}, u32[]{:S(2)}) copy-start(f32[16,32]{1,0:T(8,128)} %param.12) | copy-start | bytes 6148
  94.9 271.8 %all-to-all-start = ((bf16[248,3,4096]{0,1,2:T(4,128)(2,1)}), bf16[248,3,4096]{0,1,2:T(4,128)(2,1)}, u32[]{:S(2)}, u32[]{:S(2)}) async-start(bf16[248,3,4096]{0,1,2:T(4,128)(2,1)} %copy.193), calls=%async_computation | async-start | bytes 16777216 | tf_op jit(solution)/shard_map/all_to_all | solution.py:88
  364.9 60.9 %copy-start.6 = (bf16[1024,512]{1,0:T(8,128)(2,1)}, bf16[1024,512]{1,0:T(8,128)(2,1)S(1)}, u32[]{:S(2)}) copy-start(bf16[1024,512]{1,0:T(8,128)(2,1)S(1)} %gather_fusion.3) | copy-start | bytes 3145732
  420.0 5.8 copy-start.3
  425.8 1.7 copy-start
  427.4 1.6 copy-start.8
  430.5 28.0 %copy-start.7 = (bf16[64,8,8,128]{3,2,1,0:T(8,128)(2,1)}, bf16[64,8,8,128]{3,2,1,0:T(8,128)(2,1)S(1)}, u32[]{:S(2)}) copy-start(bf16[64,8,8,128]{3,2,1,0:T(8,128)(2,1)S(1)} %copy.250) | copy-start | bytes 3145732
  438.9 2.2 copy-start.10
  446.0 4.4 copy-start.5
  446.0 4.4 copy-start.11
  450.7 121.1 %copy-start.1 = (f32[8,128,32,16]{1,0,3,2:T(8,128)}, f32[8,128,32,16]{1,0,3,2:T(8,128)S(1)}, u32[]{:S(2)}) copy-start(f32[8,128,32,16]{1,0,3,2:T(8,128)S(1)} %convert_multiply_fusion.20) | copy-start | bytes 6291460
  450.7 3.9 copy-start.4
  472.6 5.7 copy-start.9
  487.7 2.9 copy-start.15
  520.1 84.4 %all-to-all-start.1 = ((bf16[8,2,63488]{2,1,0:T(2,128)(2,1)}), bf16[8,2,63488]{2,1,0:T(2,128)(2,1)}, u32[]{:S(2)}, u32[]{:S(2)}) async-start(bf16[8,2,63488]{2,1,0:T(2,128)(2,1)} %reshape.457), calls=%async_computation.1 | async-start | bytes 4063232 | tf_op jit(solution)/shard_map/all_to_all | solution.py:93
  588.3 4.3 copy-start.2
  604.5 182.5 %all-to-all-start.3 = ((bf16[1984,3,512]{2,1,0:T(4,128)(2,1)}), bf16[1984,3,512]{2,1,0:T(4,128)(2,1)}, u32[]{:S(2)}, u32[]{:S(2)}) async-start(bf16[1984,3,512]{2,1,0:T(4,128)(2,1)} %select_select_fusion), calls=%async_computation.3 | async-start | bytes 16252928 | tf_op jit(solution)/shard_map/all_to_all | solution.py:93
where the time goes:
time: 816 us; the launch traced here: 810 us
  local copies, waits for them, and re-layouts  281 us (34%)
  blocking collectives  193 us (24%)
  waiting for transfers between devices  167 us (20%)
  other arithmetic  91 us (11%)
  matrix products  52 us (6%)
  starting transfers between devices  22.5 us (3%)
    lt x1, blocking collectives, moved_operator(): back_valid = (slot_ids[None, :] < all_counts[:, None]).reshape(-1)  181 us
    all_to_all x2, waiting for transfers between devices, outbound(): lax.all_to_all(picked, 'ctx', split_axis=0, concat_axis=2, tiled=True)  139 us
    gather x2, local copies, waits for them, and re-layouts, modal_local(): jnp.take(kernel_rows, jnp.clip(lag_grid, 0, row_block - 1), axis=1)  60.9 us
    unnamed x60, local copies, waits for them, and re-layouts  50.1 us
    all_to_all x4, local copies, waits for them, and re-layouts, inbound(): lax.all_to_all(loader_rows, 'ctx', split_axis=2, concat_axis=0, tiled=True)  40.9 us
    gather x2, local copies, waits for them, and re-layouts, outbound(): picked = jnp.take(chan_rows, back_index, axis=0)  32.7 us
    all_to_all x2, waiting for transfers between devices, inbound(): lax.all_to_all(loader_rows, 'ctx', split_axis=2, concat_axis=0, tiled=True)  27.9 us
    unnamed x1, other arithmetic  23.6 us
  transfers between devices with their start and end apart: 4, of which 2 were waited for; matrix products, arithmetic and copies ran while one was open for 26% of the time, Pallas kernels for 0%

commit v1 on v0

--- a/solution.py
+++ b/solution.py
@@ -85,7 +85,14 @@
         return jnp.take(received, take_index, axis=0)
 
     def inbound(loader_rows):
-        return place(lax.all_to_all(loader_rows, "ctx", split_axis=2, concat_axis=0, tiled=True))
+        return place(
+            jnp.concatenate(
+                lax.all_to_all(
+                    jnp.stack(jnp.split(loader_rows, lax.axis_size("ctx"), axis=2)), "ctx", 0, 0
+                ),
+                axis=0,
+            )
+        )
 
     def outbound(chan_rows):
         picked = jnp.take(chan_rows, back_index, axis=0)

time: 816 us -> 715 us (0.88)
  blocking collectives: 193 us -> 144 us
  local copies, waits for them, and re-layouts: 281 us -> 240 us
  waiting for transfers between devices: 167 us -> 156 us
    lt x1, blocking collectives: 181 us -> 131 us  [moved_operator(): back_valid = (slot_ids[None, :] < all_counts[:, None]).reshape(-1)]
    all_to_all x4 -> x1, local copies, waits for them, and re-layouts: 40.9 us -> 10 us  [inbound(): lax.all_to_all(jnp.stack(jnp.split(loader_rows, lax.axis_size('ctx'), axi...]
    unnamed x1 -> x0, other arithmetic: 23.6 us -> none
    convert_element_type x1, other arithmetic: 5.23 us -> 20.7 us  [moved_operator(): grad_rows = outbound(d_window.astype(jnp.bfloat16))]
    all_to_all x2, waiting for transfers between devices: 27.9 us -> 17.2 us  [inbound(): lax.all_to_all(jnp.stack(jnp.split(loader_rows, lax.axis_size('ctx'), axi...]
    another operation x2 -> x3, local copies, waits for them, and re-layouts: 20.4 us -> 10.2 us  [inbound(): jnp.stack(jnp.split(loader_rows, lax.axis_size('ctx'), axis=2))]
    unnamed x60 -> x74, local copies, waits for them, and re-layouts: 50.1 us -> 50.8 us
  transfers between devices with their start and end apart: 4 -> 4, of which waited for: 2 -> 2; matrix products, arithmetic and copies ran while one was open for 26% -> 31% of each run, Pallas kernels for 0% -> 0%
where the time goes in v1:
time: 715 us; the launch traced here: 703 us
  local copies, waits for them, and re-layouts  240 us (34%)
  waiting for transfers between devices  156 us (22%)
  blocking collectives  144 us (20%)
  other arithmetic  88.1 us (12%)
  matrix products  49.9 us (7%)
  starting transfers between devices  22.7 us (3%)
    all_to_all x2, waiting for transfers between devices, outbound(): lax.all_to_all(picked, 'ctx', split_axis=0, concat_axis=2, tiled=True)  139 us
    lt x1, blocking collectives, moved_operator(): back_valid = (slot_ids[None, :] < all_counts[:, None]).reshape(-1)  131 us
    gather x2, local copies, waits for them, and re-layouts, modal_local(): jnp.take(kernel_rows, jnp.clip(lag_grid, 0, row_block - 1), axis=1)  60.9 us
    unnamed x74, local copies, waits for them, and re-layouts  50.8 us
    gather x2, local copies, waits for them, and re-layouts, outbound(): picked = jnp.take(chan_rows, back_index, axis=0)  32.4 us
    convert_element_type x1, other arithmetic, moved_operator(): grad_rows = outbound(d_window.astype(jnp.bfloat16))  20.7 us
    select_n x3, other arithmetic, outbound(): jnp.where(back_valid[:, None, None], picked, jnp.zeros_like(picked))  19.9 us
    gather x3, local copies, waits for them, and re-layouts, place(): return jnp.take(received, take_index, axis=0)  18.5 us
  transfers between devices with their start and end apart: 4, of which 2 were waited for; matrix products, arithmetic and copies ran while one was open for 31% of the time, Pallas kernels for 0%

profile of v1, /device:TPU:0, one launch (start us, length us, event | category | flops | bytes accessed | tf_op | source)
XLA Modules:
  0.0 703.1 jit_solution(7121414075707911399)
XLA Ops:
  10.3 7.3 %all-to-all-start.2 = ((bf16[8,248,1,512]{3,1,2,0:T(8,128)(2,1)}), bf16[8,248,1,512]{3,1,2,0:T(8,128)(2,1)S(1)}, u32[]{:S(2)}, u32[]{:S(2)}) async-start(bf16[8,248,1,512]{3,1,2,0:T(8,128)(2,1)} %fusion.86), calls=%async_computation.2 | async-start | bytes 4063232 | tf_op jit(solution)/shard_map/all_to_all | solution.py:90
  17.5 8.6 %copy.169 = bf16[1,1,248,12288]{2,3,1,0:T(8,128)(2,1)} copy(bf16[1,1,248,12288]{3,2,1,0:T(8,128)(2,1)} %param.9) | data formatting | bytes 12189696 | tf_op args[0]
  38.6 8.6 %copy.170 = bf16[8,248,3,512]{3,1,2,0:T(8,128)(2,1)} copy(bf16[8,248,3,512]{1,3,2,0:T(8,128)(2,1)} %fusion.70) | data formatting | bytes 12189696 | tf_op jit(solution)/shard_map/stack | solution.py:91
  47.2 17.2 %all-to-all-done.2 = bf16[8,248,1,512]{3,1,2,0:T(8,128)(2,1)S(1)} async-done(((bf16[8,248,1,512]{3,1,2,0:T(8,128)(2,1)}), bf16[8,248,1,512]{3,1,2,0:T(8,128)(2,1)S(1)}, u32[]{:S(2)}, u32[]{:S(2)}) %all-to-all-start.2) | async-done | bytes 2031648 | tf_op jit(solution)/shard_map/all_to_all | solution.py:90
  64.4 4.8 all-to-all-start
  71.1 131.3 %all-reduce.2 = s32[8]{0:T(128)S(1)} all-reduce(s32[8]{0:T(128)S(1)} %bitcast_dynamic-update-slice_fusion), channel_id=1, replica_groups=mesh['dp'=4,'ctx'=8] {'ctx'}, use_global_device_ids=true, to_apply=%add.2 | all-reduce | flops 8 | bytes 64 | tf_op jit(solution)/shard_map/lt | solution.py:82
  203.4 54.4 %gather_fusion.1 = f32[16384,32]{1,0:T(8,128)} fusion(f32[32,128]{0,1:T(8,128)S(1)} %copy.176, s32[16384]{0:T(1024)S(1)} %fusion.107), kind=kCustom, calls=%fused_computation.1 | custom fusion | bytes 4259840 | tf_op jit(solution)/shard_map/jit(_take)/gather | solution.py:24
  257.8 6.5 copy.177
  270.6 10.0 %copy.171 = bf16[8,248,3,512]{3,2,1,0:T(4,128)(2,1)} copy(bf16[8,248,3,512]{3,1,2,0:T(8,128)(2,1)} %all-to-all-done) | data formatting | bytes 12189696 | tf_op jit(solution)/shard_map/all_to_all | solution.py:90
  280.7 14.0 %gather_fusion = bf16[1024,3,512]{2,1,0:T(4,128)(2,1)} fusion(bf16[1984,3,512]{2,1,0:T(4,128)(2,1)} %bitcast.258, s32[1024]{0:T(1024)S(1)} %broadcast_clamp_fusion), kind=kCustom, calls=%fused_computation | custom fusion | bytes 6295552 | tf_op jit(solution)/shard_map/jit(_take)/gather | solution.py:85
  297.8 5.8 fusion.11
  325.1 7.7 %fusion.35 = f32[16,32,16,8]{2,3,1,0:T(8,128)} fusion(f32[8,16,32,16]{3,0,2,1:T(8,128)} %copy.179, f32[8,8]{0,1:T(8,128)S(1)} %fusion.112, f32[16,32]{1,0:T(8,128)S(1)} %get-tuple-element.118, pred[8,8]{0,1:T(8,128)(4,1)S(1)} %fusion.113), kind=kOutput, calls=%fused_computation.75 | convolution fusion | flops 6356992 | bytes 526656 | tf_op jit(solution)/shard_map/rgij,jrgq->irgq/dot_general | solution.py:41
  339.3 4.4 add_bitcast_fusion
  351.7 6.1 fusion.32
  368.0 6.1 convert_multiply_fusion.15
  374.1 9.2 %gather_fusion.2 = bf16[1984,512]{1,0:T(8,128)(2,1)} fusion(bf16[1024,512]{1,0:T(8,128)(2,1)S(1)} %get-tuple-element.108, s32[2048]{0:T(1024)S(1)} %pad_clamp_fusion), kind=kCustom, calls=%fused_computation.2 | custom fusion | bytes 4071168 | tf_op jit(solution)/shard_map/jit(_take)/gather | solution.py:98
  387.4 4.4 reduce.2
  391.8 5.9 reshape.464
  397.8 4.7 all-to-all-start.1
  402.5 16.1 %fusion.18 = (f32[3,512]{1,0:T(4,128)S(1)}, f32[3,512]{1,0:T(4,128)S(1)}, f32[3,512]{1,0:T(4,128)S(1)}, f32[3,512]{1,0:T(4,128)S(1)}, f32[3,512]{1,0:T(4,128)S(1...) fusion(bf16[1024,3,512]{2,0,1:T(8,128)(2,1)} %copy-done.3, ...), kind=kLoop, calls=%fused_computation.40 | loop fusion | flops 36165120 | bytes 15771648 | tf_op jit(solution)/shard_map/reduce_sum | solution.py:130
  418.6 14.8 %fusion.25 = f32[16,32]{0,1:T(8,128)S(1)} fusion(f32[16,32,8,16]{3,2,1,0:T(8,128)S(1)} %bitcast.257, f32[8,128,32,16]{1,0,3,2:T(8,128)S(1)} %convert_multiply_fusion.20, f32[128]{0:T(128)S(1)} %iota_add_fusion, f32[16,32]{0,1:T(8,128)S(1)} %copy.175), kind=kOutput, calls=%fused_computation.59 | convolution fusion | flops 100859392 | bytes 2363904 | tf_op jit(solution)/shard_map/iagq,rga,irgq->rg/dot_general | solution.py:58
  433.5 20.7 %add_convert_fusion = bf16[1024,3,512]{2,0,1:T(8,128)(2,1)S(1)} fusion(f32[1024,3,512]{2,0,1:T(8,128)} %get-tuple-element.106, f32[3,512]{1,0:T(4,128)S(1)} %get-tuple-element.120, f32[3,512]{1,0:T(4,128)S(1)} %get-tuple-element.121, f32[3,512]{1,0:T(4,128)S(1)} %get-tuple-element.122, f32[3,512]{1,0:T(4,128)S(1)} %get-tuple-element.123, ...), kind=kLoop, calls=%fused_computation.42 | loop fusion | flops 22020096 | bytes 9480192 | tf_op jit(solution)/shard_map/convert_element_type | solution.py:131
  454.2 4.7 copy.194
  458.9 23.3 %gather_fusion.4 = bf16[1984,3,512]{2,1,0:T(4,128)(2,1)} fusion(bf16[1024,3,512]{2,1,0:T(4,128)(2,1)} %copy.194, s32[2048]{0:T(1024)S(1)} %pad_clamp_fusion), kind=kCustom, calls=%fused_computation.4 | custom fusion | bytes 12197632 | tf_op jit(solution)/shard_map/jit(_take)/gather | solution.py:98
  486.1 11.9 %select_select_fusion = bf16[1984,3,512]{2,1,0:T(4,128)(2,1)} fusion(bf16[1984,3,512]{2,1,0:T(4,128)(2,1)S(1)} %copy-done.2, pred[1984]{0:T(1024)(128)(4,1)S(1)} %compare_and_fusion, pred[1984]{0:T(1024)(128)(4,1)S(1)} %lt.99), kind=kLoop, calls=%fused_computation.12 | loop fusion | flops 6094848 | bytes 12193664 | tf_op jit(solution)/shard_map/jit(_where)/select_n | solution.py:99
  498.0 6.0 all-to-all-start.3
  503.9 11.9 %while.11 = (s32[]{:T(128)}, f32[16,32]{1,0:T(8,128)S(1)}, f32[16,32]{1,0:T(8,128)S(1)}, f32[32,128,128]{2,1,0:T(8,128)S(1)}, s32[]{:T(128)}, /*index=5*/s32[]{:T(128)}) while((s32[]{:T(128)}, f32[16,32]{1,0:T(8,128)S(1)}, f32[16,32]{1,0:T(8,128)S(1)}, f32[32,128,128]{2,1,0:T(8,128)S(1)}, s32[]{:T(128)}, ...), condition=%wide.region_14.15_spmd.clone, body=%wide.region_12.14_spmd.clone.sunk | while | flops 2179074 | bytes 2261837 | solution.py:57
  515.9 12.5 %all-reduce.3 = (f32[7,3,512]{2,1,0:T(4,128)S(1)}, f32[16,32]{1,0:T(8,128)}, f32[512]{0:T(512)}) all-reduce(f32[7,3,512]{2,1,0:T(4,128)S(1)} %constant_dynamic-update-slice_fusion, f32[16,32]{1,0:T(8,128)S(1)} %add.246, f32[512]{0:T(512)S(1)} %get-tuple-element.99), channel_id=1, replica_groups=mesh['dp'=4,'ctx'=8] {'dp'}, use_global_device_ids=true, to_apply=%region_11.12 | all-reduce | flops 11776 | bytes 94208 | tf_op jit(solution)/shard_map/psum | solution.py:145
  529.0 6.8 reshape.465
  541.4 139.1 %all-to-all-done.3 = bf16[1984,3,512]{2,1,0:T(4,128)(2,1)} async-done(((bf16[1984,3,512]{2,1,0:T(4,128)(2,1)}), bf16[1984,3,512]{2,1,0:T(4,128)(2,1)}, u32[]{:S(2)}, u32[]{:S(2)}) %all-to-all-start.3) | async-done | bytes 6094880 | tf_op jit(solution)/shard_map/all_to_all | solution.py:100
  680.5 12.5 %copy.195 = bf16[248,3,8,512]{3,2,1,0:T(8,128)(2,1)} copy(bf16[248,3,8,512]{3,1,0,2:T(4,128)(2,1)} %bitcast.55) | data formatting | bytes 12189696 | tf_op jit(solution)/shard_map/all_to_all | solution.py:100
  693.0 9.8 %reshape.397 = bf16[1,1,248,12288]{3,2,1,0:T(8,128)(2,1)} reshape(bf16[248,3,8,512]{3,2,1,0:T(8,128)(2,1)} %copy.195) | data formatting | bytes 12189696 | tf_op jit(solution)/shard_map/reshape | solution.py:134
  (213 shorter events, 105.6 us)
Async XLA Ops:
  0.6 6.8 copy-start.13
  10.3 54.1 %all-to-all-start.2 = ((bf16[8,248,1,512]{3,1,2,0:T(8,128)(2,1)}), bf16[8,248,1,512]{3,1,2,0:T(8,128)(2,1)S(1)}, u32[]{:S(2)}, u32[]{:S(2)}) async-start(bf16[8,248,1,512]{3,1,2,0:T(8,128)(2,1)} %fusion.86), calls=%async_computation.2 | async-start | bytes 4063232 | tf_op jit(solution)/shard_map/all_to_all | solution.py:90
  26.1 8.7 %copy-start.4 = (bf16[1,1,248,12288]{2,3,1,0:T(8,128)(2,1)S(1)}, bf16[1,1,248,12288]{2,3,1,0:T(8,128)(2,1)}, u32[]{:S(2)}) copy-start(bf16[1,1,248,12288]{2,3,1,0:T(8,128)(2,1)} %copy.169) | copy-start | bytes 18284548
  47.2 22.6 %copy-start.18 = (u32[32]{0:T(128)S(1)}, u32[32]{0:T(128)}, u32[]{:S(2)}) copy-start(u32[32]{0:T(128)} %constant.117) | copy-start | bytes 388
  47.2 155.6 %copy-start.14 = (f32[7,3,512]{2,0,1:T(8,128)S(1)}, f32[7,3,512]{2,0,1:T(8,128)}, u32[]{:S(2)}) copy-start(f32[7,3,512]{2,0,1:T(8,128)} %param.11) | copy-start | bytes 129028
  47.2 155.7 %copy-start.16 = (f32[16,32]{1,0:T(8,128)S(1)}, f32[16,32]{1,0:T(8,128)}, u32[]{:S(2)}) copy-start(f32[16,32]{1,0:T(8,128)} %param.13) | copy-start | bytes 6148
  47.2 155.8 %copy-start.15 = (f32[16,32]{1,0:T(8,128)S(1)}, f32[16,32]{1,0:T(8,128)}, u32[]{:S(2)}) copy-start(f32[16,32]{1,0:T(8,128)} %param.12) | copy-start | bytes 6148
  64.4 206.3 %all-to-all-start = ((bf16[8,248,3,512]{3,1,2,0:T(8,128)(2,1)}), bf16[8,248,3,512]{3,1,2,0:T(8,128)(2,1)}, u32[]{:S(2)}, u32[]{:S(2)}) async-start(bf16[8,248,3,512]{3,1,2,0:T(8,128)(2,1)} %copy.170), calls=%async_computation | async-start | bytes 12189696 | tf_op jit(solution)/shard_map/all_to_all | solution.py:90
  268.8 36.6 %copy-start.8 = (bf16[1024,512]{1,0:T(8,128)(2,1)}, bf16[1024,512]{1,0:T(8,128)(2,1)S(1)}, u32[]{:S(2)}) copy-start(bf16[1024,512]{1,0:T(8,128)(2,1)S(1)} %gather_fusion.3) | copy-start | bytes 3145732
  297.8 5.8 copy-start.3
  303.6 2.4 copy-start
  306.6 4.1 copy-start.11
  312.0 45.8 %copy-start.9 = (bf16[64,8,8,128]{3,2,1,0:T(8,128)(2,1)}, bf16[64,8,8,128]{3,2,1,0:T(8,128)(2,1)S(1)}, u32[]{:S(2)}) copy-start(bf16[64,8,8,128]{3,2,1,0:T(8,128)(2,1)S(1)} %copy.218) | copy-start | bytes 3145732
  317.9 100.6 %copy-start.1 = (f32[8,128,32,16]{1,0,3,2:T(8,128)}, f32[8,128,32,16]{1,0,3,2:T(8,128)S(1)}, u32[]{:S(2)}) copy-start(f32[8,128,32,16]{1,0,3,2:T(8,128)S(1)} %convert_multiply_fusion.20) | copy-start | bytes 6291460
  325.1 7.7 %copy-start.12 = (f32[8,16,32,16]{3,0,2,1:T(8,128)S(1)}, f32[8,16,32,16]{3,0,2,1:T(8,128)}, u32[]{:S(2)}) copy-start(f32[8,16,32,16]{3,0,2,1:T(8,128)} %copy.190) | copy-start | bytes 786436
  332.8 4.0 copy-start.5
  351.7 6.1 copy-start.6
  365.1 2.9 copy-start.17
  397.8 100.2 %all-to-all-start.1 = ((bf16[8,2,63488]{2,1,0:T(2,128)(2,1)}), bf16[8,2,63488]{2,1,0:T(2,128)(2,1)}, u32[]{:S(2)}, u32[]{:S(2)}) async-start(bf16[8,2,63488]{2,1,0:T(2,128)(2,1)} %reshape.464), calls=%async_computation.1 | async-start | bytes 4063232 | tf_op jit(solution)/shard_map/all_to_all | solution.py:100
  402.5 16.1 %copy-start.7 = (f32[16,32,16,8]{2,3,1,0:T(8,128)S(1)}, f32[16,32,16,8]{2,3,1,0:T(8,128)}, u32[]{:S(2)}) copy-start(f32[16,32,16,8]{2,3,1,0:T(8,128)} %fusion.35) | copy-start | bytes 786436
  458.9 23.3 %copy-start.10 = (bf16[64,8,8,128]{3,2,1,0:T(8,128)(2,1)S(1)}, bf16[64,8,8,128]{3,2,1,0:T(8,128)(2,1)}, u32[]{:S(2)}) copy-start(bf16[64,8,8,128]{3,2,1,0:T(8,128)(2,1)} %copy-done.9) | copy-start | bytes 3145732
  482.1 3.9 copy-start.2
  498.0 182.5 %all-to-all-start.3 = ((bf16[1984,3,512]{2,1,0:T(4,128)(2,1)}), bf16[1984,3,512]{2,1,0:T(4,128)(2,1)}, u32[]{:S(2)}, u32[]{:S(2)}) async-start(bf16[1984,3,512]{2,1,0:T(4,128)(2,1)} %select_select_fusion), calls=%async_computation.3 | async-start | bytes 16252928 | tf_op jit(solution)/shard_map/all_to_all | solution.py:100
